TPU v7x, 32 devices: a whole 2x2x4 slice. The times are simulated.
32 devices in a mesh: chan: 16 (over z, x, core), rows: 2 (over y).
Axes of the slice: x: 2, y: 2, z: 4, core: 2. Of those that a mesh axis runs over, the one named last changes fastest.
Arguments:
- image: bfloat16 [768, 1, 32, 128], P('chan', None, 'rows'), may hold values from -3 to 3
- dw_kernel: float32 [768, 7, 7], P('chan'), may hold values from -13 to 13
- ln_gain: float32 [768], P('chan'), may hold values from 0.1 to 1.9
- w_in: bfloat16 [768, 3072], P(None, 'chan'), may hold values from -0.21875 to 0.21875
- w_out: bfloat16 [3072, 768], P('chan'), may hold values from -0.15625 to 0.15625
- layer_scale: float32 [768], P('chan'), may hold values from 0.3 to 1
- cotangent: bfloat16 [768, 1, 32, 128], P('chan', None, 'rows'), may hold values from -6 to 6
Outputs:
- block_out: bfloat16 [768, 1, 32, 128], P('chan', None, 'rows')
- grad_image: bfloat16 [768, 1, 32, 128], P('chan', None, 'rows')
- grad_kernel: float32 [768, 7, 7], P('chan')
- grad_gain: float32 [768], P('chan')
- grad_scale: float32 [768], P('chan')
- grad_w_in: float32 [768, 3072], P(None, 'chan')
- grad_w_out: float32 [3072, 768], P('chan')
All inputs are finite; a program needn't handle non-finite values.
Results may differ from a plain program's by a relative error of at most 0.018.
Values may be sent and summed in bfloat16 or wider, within the bound.
A program may use at most 64 MiB of HBM per device.

v0:
```python
import jax
import jax.numpy as jnp
from jax import lax
from jax.sharding import PartitionSpec as P

D = 768
KSIZE = 7
epsilon = 1e-06
inv_root_two = 0.7071067811865476
inv_root_two_pi = 0.3989422804014327


def extended(block, sides, width):
    for axis, dim in sides:
        count = lax.axis_size(axis)
        forward = [(i, i + 1) for i in range(count - 1)]
        backward = [(target, source) for source, target in forward]
        low = lax.ppermute(
            lax.slice_in_dim(block, block.shape[dim] - width, None, axis=dim), axis, forward
        )
        high = lax.ppermute(lax.slice_in_dim(block, 0, width, axis=dim), axis, backward)
        block = jnp.concatenate([low, block, high], axis=dim)
    return block


def gelu_slope(values):
    return (
        0.5 * (1.0 + lax.erf(values * inv_root_two))
        + values * jnp.exp(-0.5 * values * values) * inv_root_two_pi
    )


def forward_taps(padded, kernel, height, breadth):
    running = jnp.zeros((padded.shape[0], padded.shape[1], height, breadth), jnp.float32)
    for u in range(KSIZE):
        for v in range(KSIZE):
            running = (
                running
                + kernel[:, u, v][:, None, None, None]
                * padded[:, :, u : u + height, v : v + breadth]
            )
    return running


def transpose_taps(padded, kernel, height, breadth):
    running = jnp.zeros((padded.shape[0], padded.shape[1], height, breadth), jnp.float32)
    for u in range(KSIZE):
        for v in range(KSIZE):
            running = (
                running
                + kernel[:, u, v][:, None, None, None]
                * padded[:, :, 6 - u : 6 - u + height, 6 - v : 6 - v + breadth]
            )
    return running


def correlate_taps(padded, grad, height, breadth):
    columns = []
    for u in range(KSIZE):
        row_terms = []
        for v in range(KSIZE):
            row_terms.append(
                jnp.sum(grad * padded[:, :, u : u + height, v : v + breadth], axis=(1, 2, 3))
            )
        columns.append(jnp.stack(row_terms, axis=1))
    return jnp.stack(columns, axis=1)


def body(image, dw_kernel, ln_gain, w_in, w_out, layer_scale, cotangent):
    channels, images, height, breadth = image.shape
    pixels = images * height * breadth
    contract_lead = (((0,), (0,)), ((), ()))
    contract_tail = (((1,), (1,)), ((), ()))
    rimmed_image = extended(image, (("rows", 2),), 3)
    padded = jnp.pad(rimmed_image.astype(jnp.float32), ((0, 0), (0, 0), (0, 0), (3, 3)))
    mixed_in = forward_taps(padded, dw_kernel, height, breadth).astype(jnp.bfloat16)
    mixed_flat = mixed_in.reshape(channels, pixels).astype(jnp.float32)
    centre = lax.psum(jnp.sum(mixed_flat, axis=0), "chan") / D
    spread = lax.psum(jnp.sum(jnp.square(mixed_flat - centre), axis=0), "chan") / D
    inv_scale = lax.rsqrt(spread + epsilon)
    unit_norm = (mixed_flat - centre) * inv_scale
    normed = (unit_norm * ln_gain[:, None]).astype(jnp.bfloat16)
    weight_cut = w_in
    pre_act = lax.dot_general(
        weight_cut,
        lax.all_gather(normed, "chan", axis=0, tiled=True),
        contract_lead,
        preferred_element_type=jnp.float32,
    )
    activated = jax.nn.gelu(pre_act, approximate=False).astype(jnp.bfloat16)
    weight_cut = w_out
    branch = lax.psum_scatter(
        lax.dot_general(
            weight_cut, activated, contract_lead, preferred_element_type=jnp.float32
        ).astype(jnp.bfloat16),
        "chan",
        scatter_dimension=0,
        tiled=True,
    ).astype(jnp.float32)
    image_flat = image.reshape(channels, pixels).astype(jnp.float32)
    block_out = (
        (image_flat + layer_scale[:, None] * branch).astype(jnp.bfloat16).reshape(image.shape)
    )
    cotan_flat = cotangent.reshape(channels, pixels).astype(jnp.float32)
    scaled = (layer_scale[:, None] * cotan_flat).astype(jnp.bfloat16)
    portion = lax.all_gather(scaled, "chan", axis=0, tiled=True)
    weight_cut = w_out
    grad_run = jnp.dot(weight_cut, portion, preferred_element_type=jnp.float32)
    column_block = lax.dot_general(
        activated, portion, contract_tail, preferred_element_type=jnp.float32
    )
    grad_w_out = column_block
    grad_scale = jnp.sum(cotan_flat * branch, axis=1)
    grad_pre = (grad_run * gelu_slope(pre_act)).astype(jnp.bfloat16)
    grad_w_in = lax.dot_general(
        lax.all_gather(normed, "chan", axis=0, tiled=True),
        grad_pre,
        contract_tail,
        preferred_element_type=jnp.float32,
    )
    weight_cut = w_in
    grad_normed = lax.psum_scatter(
        jnp.dot(weight_cut, grad_pre, preferred_element_type=jnp.float32).astype(jnp.bfloat16),
        "chan",
        scatter_dimension=0,
        tiled=True,
    ).astype(jnp.float32)
    grad_gain = jnp.sum(grad_normed * unit_norm, axis=1)
    scaled_grad = grad_normed * ln_gain[:, None]
    total_one, total_two = lax.psum(
        (jnp.sum(scaled_grad, axis=0), jnp.sum(scaled_grad * unit_norm, axis=0)), "chan"
    )
    grad_mixed = (inv_scale * (scaled_grad - total_one / D - unit_norm * (total_two / D))).astype(
        jnp.bfloat16
    )
    grad_mixed = grad_mixed.reshape(channels, images, height, breadth)
    rimmed_grad = extended(grad_mixed, (("rows", 2),), 3)
    rimmed_grad = jnp.pad(rimmed_grad.astype(jnp.float32), ((0, 0), (0, 0), (0, 0), (3, 3)))
    spread_back = transpose_taps(rimmed_grad, dw_kernel, height, breadth)
    grad_image = (cotangent.astype(jnp.float32) + spread_back).astype(jnp.bfloat16)
    grad_kernel = correlate_taps(padded, grad_mixed.astype(jnp.float32), height, breadth)
    grad_w_in, grad_w_out, grad_kernel, grad_gain, grad_scale = (
        lax.psum(grad_w_in.astype(jnp.bfloat16), "rows").astype(jnp.float32),
        lax.psum(grad_w_out.astype(jnp.bfloat16), "rows").astype(jnp.float32),
        lax.psum(grad_kernel.astype(jnp.bfloat16), "rows").astype(jnp.float32),
        lax.psum(grad_gain.astype(jnp.bfloat16), "rows").astype(jnp.float32),
        lax.psum(grad_scale.astype(jnp.bfloat16), "rows").astype(jnp.float32),
    )
    return (block_out, grad_image, grad_kernel, grad_gain, grad_scale, grad_w_in, grad_w_out)


def solution(mesh):
    return jax.shard_map(
        body,
        mesh=mesh,
        in_specs=(
            P("chan", None, "rows", None),
            P("chan", None, None),
            P("chan"),
            P(None, "chan"),
            P("chan", None),
            P("chan"),
            P("chan", None, "rows", None),
        ),
        out_specs=(
            P("chan", None, "rows", None),
            P("chan", None, "rows", None),
            P("chan", None, None),
            P("chan"),
            P("chan"),
            P(None, "chan"),
            P("chan", None),
        ),
        check_vma=False,
    )
```

profile of v0, /device:TPU:0, one launch (start us, length us, event | category | flops | bytes accessed | tf_op | source)
XLA Modules:
  0.0 478.2 jit_solution(16257528177359169895)
XLA Ops:
  8.2 4.9 %collective-permute-start = (bf16[48,1,3,128]{3,2,1,0:T(4,128)(2,1)S(1)}, bf16[48,1,3,128]{3,2,1,0:T(4,128)(2,1)S(1)}, u32[]{:S(2)}, u32[]{:S(2)}) collective-permute-start(bf16[48,1,3,128]{3,2,1,0:T(4,128)(2,1)S(1)} %get-tuple-element.87), channel_id=1, source_target_pairs={{0,1},{2,3},{4,5},{6,7},{8,9},{10,11},{12,13},{14,15},{16,17},{18,... | collective-permute-start | bytes 110600 | tf_op jit(solution)/shard_map/ppermute | solution.py:18
  20.2 8.4 %convert_reduce_fusion = (f32[16,128]{1,0:T(8,128)S(1)}, bf16[48,1,16,128]{3,2,1,0:T(8,128)(2,1)S(1)}) fusion(f32[48]{0:T(128)} %get-tuple-element.136, f32[48]{0:T(128)} %get-tuple-element.137, f32[48]{0:T(128)S(1)} %get-tuple-element.90, f32[48,1,22,128]{3,2,1,0:T(8,128)S(1)} %maximum_convert_fusion, f32[48]{0:T(128)S(1)} %get-tuple-element.91, ...), kind=kLoop, calls=%fused_computation.340 | loop fusion | flops 9828352 | bytes 3571264 | tf_op jit(solution)/shard_map/reduce_sum | solution.py:78
  29.0 32.9 %psum.63 = f32[2048]{0:T(1024)S(1)} all-reduce(f32[2048]{0:T(1024)S(1)} %bitcast.426), channel_id=1, replica_groups=mesh['chan'=16,'rows'=2] {'chan'}, use_global_device_ids=true, to_apply=%region_1.2 | all-reduce | flops 2048 | bytes 16384 | tf_op jit(solution)/shard_map/psum | solution.py:78
  61.9 30.0 %psum.64 = f32[2048]{0:T(1024)S(1)} all-reduce(f32[2048]{0:T(1024)S(1)} %bitcast.427), channel_id=1, replica_groups=mesh['chan'=16,'rows'=2] {'chan'}, use_global_device_ids=true, to_apply=%region_3.4 | all-reduce | flops 2048 | bytes 16384 | tf_op jit(solution)/shard_map/psum | solution.py:79
  92.9 43.4 %all-gather.3.cloned.1.call-done = bf16[768,2048]{1,0:T(8,128)(2,1)} async-done(((bf16[48,2048]{1,0:T(8,128)(2,1)}), bf16[768,2048]{1,0:T(8,128)(2,1)}) %all-gather.3.cloned.1.call-update) | async-done | bytes 3145744 | tf_op jit(solution)/shard_map/all_gather | solution.py:86
  136.3 6.8 %fusion.6 = (bf16[192,2048]{1,0:T(8,128)(2,1)S(1)}, f32[192,2048]{1,0:T(8,128)}) fusion(bf16[768,192]{0,1:T(8,128)(2,1)S(1)} %copy-done, bf16[768,2048]{1,0:T(8,128)(2,1)} %all-gather.3.cloned.1.call-done), kind=kOutput, calls=%fused_computation.145 | convolution fusion | flops 629538816 | bytes 5799936 | tf_op jit(solution)/shard_map/dot_general | solution.py:84
  143.1 2.7 fusion
  145.8 4.7 copy.31
  153.0 62.7 %reduce-scatter.7.cloned.1.call-done = bf16[48,2048]{1,0:T(8,128)(2,1)} async-done(((bf16[768,2048]{1,0:T(8,128)(2,1)}), bf16[48,2048]{1,0:T(8,128)(2,1)}) %reduce-scatter.7.cloned.1.call-update) | async-done | bytes 196624
  217.7 2.6 fusion.20
  222.5 44.0 %all-gather.5.cloned.1.call-done = bf16[768,2048]{1,0:T(8,128)(2,1)} async-done(((bf16[48,2048]{1,0:T(8,128)(2,1)}), bf16[768,2048]{1,0:T(8,128)(2,1)}) %all-gather.5.cloned.1.call-update) | async-done | bytes 3145744 | tf_op jit(solution)/shard_map/all_gather | solution.py:106
  266.5 4.0 convolution_convert_fusion.2
  270.4 2.8 fusion.3
  275.3 2.7 fusion.1
  278.0 4.8 copy.33
  284.7 19.7 %all-reduce.7.cloned.1.call-done = (bf16[768,192]{0,1:T(8,128)(2,1)}, bf16[192,768]{1,0:T(8,128)(2,1)}) async-done(((bf16[768,192]{0,1:T(8,128)(2,1)}, bf16[192,768]{1,0:T(8,128)(2,1)}), (bf16[768,192]{0,1:T(8,128)(2,1)}, bf16[192,768]{1,0:T(8,128)(2,1)})) %all-reduce.7.cloned.1.call-update) | async-done | bytes 589840 | tf_op jit(solution)/shard_map/psum | solution.py:143
  308.0 66.8 %reduce-scatter.9.cloned.1.call-done = bf16[48,2048]{1,0:T(8,128)(2,1)} async-done(((bf16[768,2048]{1,0:T(8,128)(2,1)}), bf16[48,2048]{1,0:T(8,128)(2,1)}) %reduce-scatter.9.cloned.1.call-update) | async-done | bytes 196624 | tf_op jit(solution)/shard_map/reduce_scatter | solution.py:122
  376.1 57.7 %all-reduce.2 = (f32[2048]{0:T(1024)S(1)}, f32[2048]{0:T(1024)S(1)}) all-reduce(f32[2048]{0:T(1024)S(1)} %get-tuple-element.71, f32[2048]{0:T(1024)S(1)} %get-tuple-element.72), channel_id=1, replica_groups=mesh['chan'=16,'rows'=2] {'chan'}, use_global_device_ids=true, to_apply=%region_9.10 | all-reduce | flops 4096 | bytes 32768 | tf_op jit(solution)/shard_map/psum | solution.py:130
  434.9 4.3 fusion.78
  439.2 4.2 fusion.77
  443.8 2.3 fusion.76
  446.2 3.4 collective-permute-start.2
  451.1 9.2 %all-reduce.3 = (bf16[48,7,7]{0,2,1:T(8,128)(2,1)S(1)}, bf16[48]{0:T(256)(128)(2,1)S(1)}, bf16[48]{0:T(256)(128)(2,1)S(1)}) all-reduce(bf16[48,7,7]{0,2,1:T(8,128)(2,1)S(1)} %constant_dynamic-update-slice_fusion, bf16[48]{0:T(256)(128)(2,1)S(1)} %get-tuple-element.70, ...), channel_id=1, replica_groups=mesh['chan'=16,'rows'=2] {'rows'}, use_global_device_ids=true, to_apply=%region_59.60 | all-reduce | flops 2448 | bytes 9792 | tf_op jit(solution)/shard_map/psum | solution.py:145
  462.6 9.1 %fusion.166 = bf16[48,1,16,128]{3,2,1,0:T(8,128)(2,1)} fusion(f32[48,1,22,128]{3,2,1,0:T(8,128)S(1)} %maximum_convert_fusion.1, f32[48]{0:T(128)} %get-tuple-element.136, f32[48]{0:T(128)} %get-tuple-element.137, f32[48]{0:T(128)S(1)} %get-tuple-element.90, f32[48]{0:T(128)S(1)} %get-tuple-element.91, f32[48]{0:T(128)S(1)} %get-tuple-element.92, ...), kind=kLoop, calls=%fused_computation.320 | loop fusion | flops 9830400 | bytes 3759680 | tf_op jit(solution)/shard_map/convert_element_type | solution.py:140
  (231 shorter events, 29.0 us)
Async XLA Ops:
  7.2 129.1 %copy-start = (bf16[768,192]{0,1:T(8,128)(2,1)S(1)}, bf16[768,192]{0,1:T(8,128)(2,1)}, u32[]{:S(2)}) copy-start(bf16[768,192]{0,1:T(8,128)(2,1)} %param.10) | copy-start | bytes 884740
  7.2 129.1 %all-gather.3.cloned.1.call-start = ((), (), s32[]{:S(2)}) async-start(), calls=%async_computation.2 | async-start | bytes 3342336 | tf_op jit(solution)/shard_map/all_gather | solution.py:86
  8.2 10.0 %collective-permute-start = (bf16[48,1,3,128]{3,2,1,0:T(4,128)(2,1)S(1)}, bf16[48,1,3,128]{3,2,1,0:T(4,128)(2,1)S(1)}, u32[]{:S(2)}, u32[]{:S(2)}) collective-permute-start(bf16[48,1,3,128]{3,2,1,0:T(4,128)(2,1)S(1)} %get-tuple-element.87), channel_id=1, source_target_pairs={{0,1},{2,3},{4,5},{6,7},{8,9},{10,11},{12,13},{14,15},{16,17},{18,... | collective-permute-start | bytes 110600 | tf_op jit(solution)/shard_map/ppermute | solution.py:18
  13.1 6.0 %collective-permute-start.1 = (bf16[48,1,3,128]{3,2,1,0:T(4,128)(2,1)S(1)}, bf16[48,1,3,128]{3,2,1,0:T(4,128)(2,1)S(1)}, u32[]{:S(2)}, u32[]{:S(2)}) collective-permute-start(bf16[48,1,3,128]{3,2,1,0:T(4,128)(2,1)S(1)} %get-tuple-element.88), channel_id=1, source_target_pairs={{1,0},{3,2},{5,4},{7,6},{9,8},{11,10},{13,12},{15,14},{17,16},{19,... | collective-permute-start | bytes 110600 | tf_op jit(solution)/shard_map/ppermute | solution.py:21
  20.2 71.8 %copy-start.7 = (f32[48]{0:T(128)S(1)}, f32[48]{0:T(128)}, u32[]{:S(2)}) copy-start(f32[48]{0:T(128)} %param.9) | copy-start | bytes 580
  92.8 50.3 %copy-start.5 = (bf16[192,768]{1,0:T(8,128)(2,1)S(1)}, bf16[192,768]{1,0:T(8,128)(2,1)}, u32[]{:S(2)}) copy-start(bf16[192,768]{1,0:T(8,128)(2,1)} %param.11) | copy-start | bytes 884740
  92.8 122.9 %reduce-scatter.7.cloned.1.call-start = ((), (), s32[]{:S(2)}) async-start(), calls=%async_computation.4 | async-start | bytes 3342336
  150.5 115.9 %all-gather.5.cloned.1.call-start = ((), (), s32[]{:S(2)}) async-start(), calls=%async_computation.3 | async-start | bytes 3342336 | tf_op jit(solution)/shard_map/all_gather | solution.py:106
  222.2 48.2 %copy-start.6 = (bf16[192,768]{1,0:T(8,128)(2,1)S(1)}, bf16[192,768]{1,0:T(8,128)(2,1)}, u32[]{:S(2)}) copy-start(bf16[192,768]{1,0:T(8,128)(2,1)} %param.11) | copy-start | bytes 884740
  222.2 82.2 %all-reduce.7.cloned.1.call-start = ((), (), s32[]{:S(2)}) async-start(), calls=%async_computation.6 | async-start | bytes 1179648 | tf_op jit(solution)/shard_map/psum | solution.py:143
  275.2 99.6 %reduce-scatter.9.cloned.1.call-start = ((), (), s32[]{:S(2)}) async-start(), calls=%async_computation.5 | async-start | bytes 3342336 | tf_op jit(solution)/shard_map/reduce_scatter | solution.py:122
  443.4 18.8 %copy-start.9 = (f32[48]{0:T(128)S(1)}, f32[48]{0:T(128)}, u32[]{:S(2)}) copy-start(f32[48]{0:T(128)} %copy-done.8) | copy-start | bytes 580
  443.4 18.8 %copy-start.11 = (f32[48]{0:T(128)S(1)}, f32[48]{0:T(128)}, u32[]{:S(2)}) copy-start(f32[48]{0:T(128)} %copy-done.10) | copy-start | bytes 580
  443.4 18.8 %copy-start.13 = (f32[48]{0:T(128)S(1)}, f32[48]{0:T(128)}, u32[]{:S(2)}) copy-start(f32[48]{0:T(128)} %copy-done.12) | copy-start | bytes 580
  443.4 18.8 %copy-start.15 = (f32[48]{0:T(128)S(1)}, f32[48]{0:T(128)}, u32[]{:S(2)}) copy-start(f32[48]{0:T(128)} %copy-done.14) | copy-start | bytes 580
  443.5 18.8 %copy-start.17 = (f32[48]{0:T(128)S(1)}, f32[48]{0:T(128)}, u32[]{:S(2)}) copy-start(f32[48]{0:T(128)} %copy-done.16) | copy-start | bytes 580
  443.5 18.8 %copy-start.19 = (f32[48]{0:T(128)S(1)}, f32[48]{0:T(128)}, u32[]{:S(2)}) copy-start(f32[48]{0:T(128)} %copy-done.18) | copy-start | bytes 580
  443.5 18.8 %copy-start.21 = (f32[48]{0:T(128)S(1)}, f32[48]{0:T(128)}, u32[]{:S(2)}) copy-start(f32[48]{0:T(128)} %copy-done.20) | copy-start | bytes 580
  443.5 18.8 %copy-start.23 = (f32[48]{0:T(128)S(1)}, f32[48]{0:T(128)}, u32[]{:S(2)}) copy-start(f32[48]{0:T(128)} %copy-done.22) | copy-start | bytes 580
  443.5 18.8 %copy-start.25 = (f32[48]{0:T(128)S(1)}, f32[48]{0:T(128)}, u32[]{:S(2)}) copy-start(f32[48]{0:T(128)} %copy-done.24) | copy-start | bytes 580
  443.5 18.8 %copy-start.27 = (f32[48]{0:T(128)S(1)}, f32[48]{0:T(128)}, u32[]{:S(2)}) copy-start(f32[48]{0:T(128)} %copy-done.26) | copy-start | bytes 580
  443.5 18.8 %copy-start.29 = (f32[48]{0:T(128)S(1)}, f32[48]{0:T(128)}, u32[]{:S(2)}) copy-start(f32[48]{0:T(128)} %copy-done.28) | copy-start | bytes 580
  446.2 15.8 %collective-permute-start.2 = (bf16[48,1,3,128]{3,2,1,0:T(4,128)(2,1)S(1)}, bf16[48,1,3,128]{3,2,1,0:T(4,128)(2,1)S(1)}, u32[]{:S(2)}, u32[]{:S(2)}) collective-permute-start(bf16[48,1,3,128]{3,2,1,0:T(4,128)(2,1)S(1)} %get-tuple-element.85), channel_id=1, source_target_pairs={{0,1},{2,3},{4,5},{6,7},{8,9},{10,11},{12,13},{14,15},{16,17},{18,... | collective-permute-start | bytes 110600 | tf_op jit(solution)/shard_map/ppermute | solution.py:18
  449.6 12.4 %collective-permute-start.3 = (bf16[48,1,3,128]{3,2,1,0:T(4,128)(2,1)S(1)}, bf16[48,1,3,128]{3,2,1,0:T(4,128)(2,1)S(1)}, u32[]{:S(2)}, u32[]{:S(2)}) collective-permute-start(bf16[48,1,3,128]{3,2,1,0:T(4,128)(2,1)S(1)} %get-tuple-element.86), channel_id=1, source_target_pairs={{1,0},{3,2},{5,4},{7,6},{9,8},{11,10},{13,12},{15,14},{17,16},{19,... | collective-permute-start | bytes 110600 | tf_op jit(solution)/shard_map/ppermute | solution.py:21
  (72 other events, 1009.5 us)
Sparse Core Ops, SparseCore 0:
  92.9 43.3 all-gather.2
  150.7 65.0 reduce-scatter.6
  222.3 44.0 all-gather.4
  275.3 29.0 all-reduce.6
  308.5 66.2 reduce-scatter.8
where the time goes:
time: 479 us; the launch traced here: 478 us
  waiting for transfers between devices  238 us (50%)
  blocking collectives  130 us (27%)
  other arithmetic  40.6 us (8%)
  local copies, waits for them, and re-layouts  22.8 us (5%)
  matrix products  21 us (4%)
  between operations  15.2 us (3%)
  starting transfers between devices  11.2 us (2%)
    reduce_scatter x1, waiting for transfers between devices, body(): lax.psum_scatter(jnp.dot(weight_cut, grad_pre, preferred_element_type=jnp...  66.8 us
    unnamed x6, waiting for transfers between devices  62.8 us
    psum x1, blocking collectives, body(): lax.psum((jnp.sum(scaled_grad, axis=0), jnp.sum(scaled_grad * unit_norm,...  57.7 us
    all_gather x1, waiting for transfers between devices, body(): portion = lax.all_gather(scaled, 'chan', axis=0, tiled=True)  44 us
    all_gather x1, waiting for transfers between devices, body(): lax.all_gather(normed, 'chan', axis=0, tiled=True)  43.4 us
    psum x1, blocking collectives, body(): centre = lax.psum(jnp.sum(mixed_flat, axis=0), 'chan') / D  32.9 us
    psum x1, blocking collectives, body(): lax.psum(jnp.sum(jnp.square(mixed_flat - centre), axis=0), 'chan') / D  30 us
    psum x1, waiting for transfers between devices, body(): lax.psum(grad_w_in.astype(jnp.bfloat16), 'rows').astype(jnp.float32)  19.7 us
  transfers between devices with their start and end apart: 9, of which 6 were waited for; matrix products, arithmetic and copies ran while one was open for 4% of the time, Pallas kernels for 0%

commit v1 on v0

--- a/solution.py
+++ b/solution.py
@@ -8,6 +8,40 @@
 epsilon = 1e-06
 inv_root_two = 0.7071067811865476
 inv_root_two_pi = 0.3989422804014327
+
+
+def fill_records(block_in):
+    axis_id = "chan"
+    state_now, aux, block_next = (
+        jax.lax.axis_size(axis_id),
+        jax.lax.axis_index(axis_id),
+        block_in.shape[0],
+    )
+    a_next = lax.dynamic_update_slice_in_dim(
+        jnp.zeros(
+            [nth * state_now if p == 0 else nth for p, nth in enumerate(block_in.shape)],
+            block_in.dtype,
+        ),
+        block_in,
+        aux * block_next,
+        axis=0,
+    )
+    kept_arr = response = block_in
+    for i0 in range(1, state_now // 2 + 1):
+        kept_arr = jax.lax.ppermute(
+            kept_arr, axis_name=axis_id, perm=[(p, (p + 1) % state_now) for p in range(state_now)]
+        )
+        a_next = lax.dynamic_update_slice_in_dim(
+            a_next, kept_arr, (aux - i0) % state_now * block_next, axis=0
+        )
+        if 2 * i0 < state_now:
+            response = jax.lax.ppermute(
+                response, axis_id, [(p, (p - 1) % state_now) for p in range(state_now)]
+            )
+            a_next = lax.dynamic_update_slice_in_dim(
+                a_next, response, (aux + i0) % state_now * block_next, axis=0
+            )
+    return a_next
 
 
 def extended(block, sides, width):
@@ -82,10 +116,7 @@
     normed = (unit_norm * ln_gain[:, None]).astype(jnp.bfloat16)
     weight_cut = w_in
     pre_act = lax.dot_general(
-        weight_cut,
-        lax.all_gather(normed, "chan", axis=0, tiled=True),
-        contract_lead,
-        preferred_element_type=jnp.float32,
+        weight_cut, fill_records(normed), contract_lead, preferred_element_type=jnp.float32
     )
     activated = jax.nn.gelu(pre_act, approximate=False).astype(jnp.bfloat16)
     weight_cut = w_out

time: 479 us -> 687 us (1.43)
  local copies, waits for them, and re-layouts: 22.8 us -> 133 us
  starting transfers between devices: 11.2 us -> 65.8 us
  waiting for transfers between devices: 238 us -> 271 us
    dynamic_update_slice x0 -> x16, local copies, waits for them, and re-layouts: none -> 104 us  [the longest x8 51.1 us: fill_records(): lax.dynamic_update_slice_in_dim(a_next, kept_arr, (aux - i0) % state_now...]
    reduce_scatter x1 -> x0, waiting for transfers between devices: 66.8 us -> none  [body(): lax.psum_scatter(jnp.dot(weight_cut, grad_pre, preferred_element_type=jnp...]
    unnamed x6 -> x7, waiting for transfers between devices: 62.8 us -> 129 us
    ppermute x0 -> x15, starting transfers between devices: none -> 54.8 us  [the longest x8 42.4 us: fill_records(): jax.lax.ppermute(kept_arr, axis_name=axis_id, perm=[(p, (p + 1) % state_n...]
    ppermute x0 -> x15, waiting for transfers between devices: none -> 37.5 us  [the longest x8 37.5 us: fill_records(): jax.lax.ppermute(kept_arr, axis_name=axis_id, perm=[(p, (p + 1) % state_n...]
    unnamed x185 -> x215, local copies, waits for them, and re-layouts: 14.6 us -> 16.1 us
  transfers between devices with their start and end apart: 9 -> 24, of which waited for: 6 -> 13; matrix products, arithmetic and copies ran while one was open for 4% -> 19% of each run, Pallas kernels for 0% -> 0%
where the time goes in v1:
time: 687 us; the launch traced here: 680 us
  waiting for transfers between devices  271 us (39%)
  local copies, waits for them, and re-layouts  133 us (19%)
  blocking collectives  130 us (19%)
  starting transfers between devices  65.8 us (10%)
  other arithmetic  41.1 us (6%)
  matrix products  22.9 us (3%)
  between operations  15.5 us (2%)
    unnamed x7, waiting for transfers between devices  129 us
    psum x1, blocking collectives, body(): lax.psum((jnp.sum(scaled_grad, axis=0), jnp.sum(scaled_grad * unit_norm,...  58 us
    dynamic_update_slice x8, local copies, waits for them, and re-layouts, fill_records(): lax.dynamic_update_slice_in_dim(a_next, kept_arr, (aux - i0) % state_now...  51.1 us
    dynamic_update_slice x7, local copies, waits for them, and re-layouts, fill_records(): lax.dynamic_update_slice_in_dim(a_next, response, (aux + i0) % state_now...  46.5 us
    all_gather x1, waiting for transfers between devices, body(): portion = lax.all_gather(scaled, 'chan', axis=0, tiled=True)  43.2 us
    ppermute x8, starting transfers between devices, fill_records(): jax.lax.ppermute(kept_arr, axis_name=axis_id, perm=[(p, (p + 1) % state_n...  42.4 us
    all_gather x1, waiting for transfers between devices, body(): lax.all_gather(normed, 'chan', axis=0, tiled=True)  40.5 us
    ppermute x8, waiting for transfers between devices, fill_records(): jax.lax.ppermute(kept_arr, axis_name=axis_id, perm=[(p, (p + 1) % state_n...  37.5 us
  transfers between devices with their start and end apart: 24, of which 13 were waited for; matrix products, arithmetic and copies ran while one was open for 19% of the time, Pallas kernels for 0%

profile of v1, /device:TPU:0, one launch (start us, length us, event | category | flops | bytes accessed | tf_op | source)
XLA Modules:
  0.0 679.6 jit_solution(9682842674159667044)
XLA Ops:
  20.2 8.3 %convert_reduce_fusion = (f32[16,128]{1,0:T(8,128)S(1)}, bf16[48,1,16,128]{3,2,1,0:T(8,128)(2,1)S(1)}) fusion(f32[48]{0:T(128)} %get-tuple-element.136, f32[48]{0:T(128)} %get-tuple-element.137, f32[48]{0:T(128)S(1)} %get-tuple-element.90, f32[48,1,22,128]{3,2,1,0:T(8,128)S(1)} %maximum_convert_fusion, f32[48]{0:T(128)S(1)} %get-tuple-element.91, ...), kind=kLoop, calls=%fused_computation.339 | loop fusion | flops 9828352 | bytes 3571264 | tf_op jit(solution)/shard_map/reduce_sum | solution.py:112
  28.9 32.8 %psum.63 = f32[2048]{0:T(1024)S(1)} all-reduce(f32[2048]{0:T(1024)S(1)} %bitcast.312), channel_id=1, replica_groups=mesh['chan'=16,'rows'=2] {'chan'}, use_global_device_ids=true, to_apply=%region_1.2 | all-reduce | flops 2048 | bytes 16384 | tf_op jit(solution)/shard_map/psum | solution.py:112
  62.1 30.0 %psum.64 = f32[2048]{0:T(1024)S(1)} all-reduce(f32[2048]{0:T(1024)S(1)} %bitcast.313), channel_id=1, replica_groups=mesh['chan'=16,'rows'=2] {'chan'}, use_global_device_ids=true, to_apply=%region_3.4 | all-reduce | flops 2048 | bytes 16384 | tf_op jit(solution)/shard_map/psum | solution.py:113
  97.3 7.0 %collective-permute-done.2 = bf16[48,2048]{0,1:T(8,128)(2,1)S(1)} collective-permute-done((bf16[48,2048]{0,1:T(8,128)(2,1)S(1)}, bf16[48,2048]{0,1:T(8,128)(2,1)S(1)}, u32[]{:S(2)}, u32[]{:S(2)}) %collective-permute-start.2) | collective-permute-done | bytes 196640 | tf_op jit(solution)/shard_map/ppermute | solution.py:31
  108.7 7.0 %collective-permute-done.4 = bf16[48,2048]{0,1:T(8,128)(2,1)S(1)} collective-permute-done((bf16[48,2048]{0,1:T(8,128)(2,1)S(1)}, bf16[48,2048]{0,1:T(8,128)(2,1)S(1)}, u32[]{:S(2)}, u32[]{:S(2)}) %collective-permute-start.4) | collective-permute-done | bytes 196640 | tf_op jit(solution)/shard_map/ppermute | solution.py:31
  120.1 6.8 %collective-permute-done.6 = bf16[48,2048]{0,1:T(8,128)(2,1)S(1)} collective-permute-done((bf16[48,2048]{0,1:T(8,128)(2,1)S(1)}, bf16[48,2048]{0,1:T(8,128)(2,1)S(1)}, u32[]{:S(2)}, u32[]{:S(2)}) %collective-permute-start.6) | collective-permute-done | bytes 196640 | tf_op jit(solution)/shard_map/ppermute | solution.py:31
  131.5 6.9 %collective-permute-done.8 = bf16[48,2048]{0,1:T(8,128)(2,1)S(1)} collective-permute-done((bf16[48,2048]{0,1:T(8,128)(2,1)S(1)}, bf16[48,2048]{0,1:T(8,128)(2,1)S(1)}, u32[]{:S(2)}, u32[]{:S(2)}) %collective-permute-start.8) | collective-permute-done | bytes 196640 | tf_op jit(solution)/shard_map/ppermute | solution.py:31
  138.4 7.1 %collective-permute-start.10 = (bf16[48,2048]{0,1:T(8,128)(2,1)S(1)}, bf16[48,2048]{0,1:T(8,128)(2,1)S(1)}, u32[]{:S(2)}, u32[]{:S(2)}) collective-permute-start(bf16[48,2048]{0,1:T(8,128)(2,1)S(1)} %collective-permute-done.8), channel_id=1, source_target_pairs={{0,2},{2,4},{4,6},{6,8},{8,10},{10,12},{12,14},{14,16},{16,18},{18... | collective-permute-start | bytes 589832 | tf_op jit(solution)/shard_map/ppermute | solution.py:31
  149.8 9.9 %collective-permute-start.12 = (bf16[48,2048]{0,1:T(8,128)(2,1)S(1)}, bf16[48,2048]{0,1:T(8,128)(2,1)S(1)}, u32[]{:S(2)}, u32[]{:S(2)}) collective-permute-start(bf16[48,2048]{0,1:T(8,128)(2,1)S(1)} %collective-permute-done.10), channel_id=1, source_target_pairs={{0,2},{2,4},{4,6},{6,8},{8,10},{10,12},{12,14},{14,16},{16,18},{18... | collective-permute-start | bytes 589832 | tf_op jit(solution)/shard_map/ppermute | solution.py:31
  162.5 11.4 %collective-permute-start.14 = (bf16[48,2048]{0,1:T(8,128)(2,1)S(1)}, bf16[48,2048]{0,1:T(8,128)(2,1)}, u32[]{:S(2)}, u32[]{:S(2)}) collective-permute-start(bf16[48,2048]{0,1:T(8,128)(2,1)S(1)} %collective-permute-done.12), channel_id=1, source_target_pairs={{0,2},{2,4},{4,6},{6,8},{8,10},{10,12},{12,14},{14,16},{16,18},{18... | collective-permute-start | bytes 589832 | tf_op jit(solution)/shard_map/ppermute | solution.py:31
  176.8 8.3 %collective-permute-start.16 = (bf16[48,2048]{0,1:T(8,128)(2,1)}, bf16[48,2048]{0,1:T(8,128)(2,1)}, u32[]{:S(2)}, u32[]{:S(2)}) collective-permute-start(bf16[48,2048]{0,1:T(8,128)(2,1)} %collective-permute-done.14), channel_id=1, source_target_pairs={{0,2},{2,4},{4,6},{6,8},{8,10},{10,12},{12,14},{14,16},{16,18},{18... | collective-permute-start | bytes 589832 | tf_op jit(solution)/shard_map/ppermute | solution.py:31
  224.8 6.8 %dynamic_update_slice.54 = bf16[768,2048]{0,1:T(8,128)(2,1)} dynamic-update-slice(bf16[768,2048]{0,1:T(8,128)(2,1)} %dynamic_update_slice.53, bf16[48,2048]{0,1:T(8,128)(2,1)} %copy-done.10, s32[]{:T(128)S(6)} %select_n.123, s32[]{:T(128)} %constant.137.clone.1) | dynamic-update-slice | bytes 393220 | tf_op jit(solution)/shard_map/dynamic_update_slice | solution.py:41
  244.6 6.8 %dynamic_update_slice.57 = bf16[768,2048]{0,1:T(8,128)(2,1)} dynamic-update-slice(bf16[768,2048]{0,1:T(8,128)(2,1)} %dynamic_update_slice.56, bf16[48,2048]{0,1:T(8,128)(2,1)} %copy-done.15, s32[]{:T(128)S(6)} %select_n.129, s32[]{:T(128)} %constant.137.clone.1) | dynamic-update-slice | bytes 393220 | tf_op jit(solution)/shard_map/dynamic_update_slice | solution.py:34
  271.2 6.8 %dynamic_update_slice.61 = bf16[768,2048]{0,1:T(8,128)(2,1)} dynamic-update-slice(bf16[768,2048]{0,1:T(8,128)(2,1)} %dynamic_update_slice.60, bf16[48,2048]{0,1:T(8,128)(2,1)} %collective-permute-done.14, s32[]{:T(128)S(6)} %select_n.137, s32[]{:T(128)} %constant.137.clone.1) | dynamic-update-slice | bytes 393220 | tf_op jit(solution)/shard_map/dynamic_update_slice | solution.py:34
  278.0 6.8 %dynamic_update_slice.62 = bf16[768,2048]{0,1:T(8,128)(2,1)} dynamic-update-slice(bf16[768,2048]{0,1:T(8,128)(2,1)} %dynamic_update_slice.61, bf16[48,2048]{0,1:T(8,128)(2,1)} %collective-permute-done.15, s32[]{:T(128)S(6)} %select_n.139, s32[]{:T(128)} %constant.137.clone.1) | dynamic-update-slice | bytes 393220 | tf_op jit(solution)/shard_map/dynamic_update_slice | solution.py:41
  290.8 7.0 %fusion.6 = (bf16[192,2048]{1,0:T(8,128)(2,1)S(1)}, f32[192,2048]{1,0:T(8,128)}) fusion(bf16[768,2048]{0,1:T(8,128)(2,1)} %dynamic_update_slice.63, bf16[768,192]{0,1:T(8,128)(2,1)S(1)} %copy-done), kind=kOutput, calls=%fused_computation.145 | convolution fusion | flops 629538816 | bytes 5799936 | tf_op jit(solution)/shard_map/dot_general | solution.py:118
  309.9 62.3 %reduce-scatter.7.cloned.1.call-done = bf16[48,2048]{1,0:T(8,128)(2,1)} async-done(((bf16[768,2048]{1,0:T(8,128)(2,1)}), bf16[48,2048]{1,0:T(8,128)(2,1)}) %reduce-scatter.7.cloned.1.call-update) | async-done | bytes 196624
  380.1 43.2 %all-gather.3.cloned.1.call-done = bf16[768,2048]{1,0:T(8,128)(2,1)} async-done(((bf16[48,2048]{1,0:T(8,128)(2,1)}), bf16[768,2048]{1,0:T(8,128)(2,1)}) %all-gather.3.cloned.1.call-update) | async-done | bytes 3145744 | tf_op jit(solution)/shard_map/all_gather | solution.py:137
  429.9 40.5 %all-gather.5.cloned.1.call-done = bf16[768,2048]{1,0:T(8,128)(2,1)} async-done(((bf16[48,2048]{1,0:T(8,128)(2,1)}), bf16[768,2048]{1,0:T(8,128)(2,1)}) %all-gather.5.cloned.1.call-update) | async-done | bytes 3145744 | tf_op jit(solution)/shard_map/all_gather | solution.py:147
  483.8 19.7 %all-reduce.7.cloned.1.call-done = (bf16[768,192]{0,1:T(8,128)(2,1)}, bf16[192,768]{1,0:T(8,128)(2,1)}) async-done(((bf16[768,192]{0,1:T(8,128)(2,1)}, bf16[192,768]{1,0:T(8,128)(2,1)}), (bf16[768,192]{0,1:T(8,128)(2,1)}, bf16[192,768]{1,0:T(8,128)(2,1)})) %all-reduce.7.cloned.1.call-update) | async-done | bytes 589840 | tf_op jit(solution)/shard_map/psum | solution.py:174
  507.1 66.8 %reduce-scatter.9.cloned.1.call-done = bf16[48,2048]{1,0:T(8,128)(2,1)} async-done(((bf16[768,2048]{1,0:T(8,128)(2,1)}), bf16[48,2048]{1,0:T(8,128)(2,1)}) %reduce-scatter.9.cloned.1.call-update) | async-done | bytes 196624
  576.5 58.0 %all-reduce.2 = (f32[2048]{0:T(1024)S(1)}, f32[2048]{0:T(1024)S(1)}) all-reduce(f32[2048]{0:T(1024)S(1)} %get-tuple-element.22, f32[2048]{0:T(1024)S(1)} %get-tuple-element.72), channel_id=1, replica_groups=mesh['chan'=16,'rows'=2] {'chan'}, use_global_device_ids=true, to_apply=%region_9.10 | all-reduce | flops 4096 | bytes 32768 | tf_op jit(solution)/shard_map/psum | solution.py:161
  652.3 9.2 %all-reduce.3 = (bf16[48,7,7]{0,2,1:T(8,128)(2,1)S(1)}, bf16[48]{0:T(256)(128)(2,1)S(1)}, bf16[48]{0:T(256)(128)(2,1)S(1)}) all-reduce(bf16[48,7,7]{0,2,1:T(8,128)(2,1)S(1)} %constant_dynamic-update-slice_fusion, bf16[48]{0:T(256)(128)(2,1)S(1)} %get-tuple-element.21, ...), channel_id=1, replica_groups=mesh['chan'=16,'rows'=2] {'rows'}, use_global_device_ids=true, to_apply=%region_59.60 | all-reduce | flops 2448 | bytes 9792 | tf_op jit(solution)/shard_map/psum | solution.py:176
  663.8 9.1 %fusion.167 = bf16[48,1,16,128]{3,2,1,0:T(8,128)(2,1)} fusion(f32[48,1,22,128]{3,2,1,0:T(8,128)S(1)} %maximum_convert_fusion.1, f32[48]{0:T(128)} %get-tuple-element.136, f32[48]{0:T(128)} %get-tuple-element.137, f32[48]{0:T(128)S(1)} %get-tuple-element.90, f32[48]{0:T(128)S(1)} %get-tuple-element.91, f32[48]{0:T(128)S(1)} %get-tuple-element.92, ...), kind=kLoop, calls=%fused_computation.323 | loop fusion | flops 9830400 | bytes 3759680 | tf_op jit(solution)/shard_map/convert_element_type | solution.py:171
  (310 shorter events, 185.4 us)
Async XLA Ops:
  7.2 365.1 %reduce-scatter.7.cloned.1.call-start = ((), (), s32[]{:S(2)}) async-start(), calls=%async_computation.4 | async-start | bytes 3342336
  8.3 10.0 %collective-permute-start = (bf16[48,1,3,128]{3,2,1,0:T(4,128)(2,1)S(1)}, bf16[48,1,3,128]{3,2,1,0:T(4,128)(2,1)S(1)}, u32[]{:S(2)}, u32[]{:S(2)}) collective-permute-start(bf16[48,1,3,128]{3,2,1,0:T(4,128)(2,1)S(1)} %get-tuple-element.87), channel_id=1, source_target_pairs={{0,1},{2,3},{4,5},{6,7},{8,9},{10,11},{12,13},{14,15},{16,17},{18,... | collective-permute-start | bytes 110600 | tf_op jit(solution)/shard_map/ppermute | solution.py:52
  13.1 6.0 collective-permute-start.1
  92.8 11.5 %collective-permute-start.2 = (bf16[48,2048]{0,1:T(8,128)(2,1)S(1)}, bf16[48,2048]{0,1:T(8,128)(2,1)S(1)}, u32[]{:S(2)}, u32[]{:S(2)}) collective-permute-start(bf16[48,2048]{0,1:T(8,128)(2,1)S(1)} %multiply_convert_fusion), channel_id=1, source_target_pairs={{0,2},{2,4},{4,6},{6,8},{8,10},{10,12},{12,14},{14,16},{16,18},{18... | collective-permute-start | bytes 589832 | tf_op jit(solution)/shard_map/ppermute | solution.py:31
  92.8 11.4 %collective-permute-start.3 = (bf16[48,2048]{0,1:T(8,128)(2,1)S(1)}, bf16[48,2048]{0,1:T(8,128)(2,1)S(1)}, u32[]{:S(2)}, u32[]{:S(2)}) collective-permute-start(bf16[48,2048]{0,1:T(8,128)(2,1)S(1)} %multiply_convert_fusion), channel_id=1, source_target_pairs={{0,30},{2,0},{4,2},{6,4},{8,6},{10,8},{12,10},{14,12},{16,14},{18,... | collective-permute-start | bytes 589832 | tf_op jit(solution)/shard_map/ppermute | solution.py:38
  104.2 11.4 %collective-permute-start.4 = (bf16[48,2048]{0,1:T(8,128)(2,1)S(1)}, bf16[48,2048]{0,1:T(8,128)(2,1)S(1)}, u32[]{:S(2)}, u32[]{:S(2)}) collective-permute-start(bf16[48,2048]{0,1:T(8,128)(2,1)S(1)} %collective-permute-done.2), channel_id=1, source_target_pairs={{0,2},{2,4},{4,6},{6,8},{8,10},{10,12},{12,14},{14,16},{16,18},{18... | collective-permute-start | bytes 589832 | tf_op jit(solution)/shard_map/ppermute | solution.py:31
  104.2 12.8 %collective-permute-start.5 = (bf16[48,2048]{0,1:T(8,128)(2,1)S(1)}, bf16[48,2048]{0,1:T(8,128)(2,1)S(1)}, u32[]{:S(2)}, u32[]{:S(2)}) collective-permute-start(bf16[48,2048]{0,1:T(8,128)(2,1)S(1)} %collective-permute-done.3), channel_id=1, source_target_pairs={{0,30},{2,0},{4,2},{6,4},{8,6},{10,8},{12,10},{14,12},{16,14},{18,... | collective-permute-start | bytes 589832 | tf_op jit(solution)/shard_map/ppermute | solution.py:38
  115.6 11.3 %collective-permute-start.6 = (bf16[48,2048]{0,1:T(8,128)(2,1)S(1)}, bf16[48,2048]{0,1:T(8,128)(2,1)S(1)}, u32[]{:S(2)}, u32[]{:S(2)}) collective-permute-start(bf16[48,2048]{0,1:T(8,128)(2,1)S(1)} %collective-permute-done.4), channel_id=1, source_target_pairs={{0,2},{2,4},{4,6},{6,8},{8,10},{10,12},{12,14},{14,16},{16,18},{18... | collective-permute-start | bytes 589832 | tf_op jit(solution)/shard_map/ppermute | solution.py:31
  117.0 14.2 %collective-permute-start.7 = (bf16[48,2048]{0,1:T(8,128)(2,1)S(1)}, bf16[48,2048]{0,1:T(8,128)(2,1)S(1)}, u32[]{:S(2)}, u32[]{:S(2)}) collective-permute-start(bf16[48,2048]{0,1:T(8,128)(2,1)S(1)} %collective-permute-done.5), channel_id=1, source_target_pairs={{0,30},{2,0},{4,2},{6,4},{8,6},{10,8},{12,10},{14,12},{16,14},{18,... | collective-permute-start | bytes 589832 | tf_op jit(solution)/shard_map/ppermute | solution.py:38
  127.0 11.4 %collective-permute-start.8 = (bf16[48,2048]{0,1:T(8,128)(2,1)S(1)}, bf16[48,2048]{0,1:T(8,128)(2,1)S(1)}, u32[]{:S(2)}, u32[]{:S(2)}) collective-permute-start(bf16[48,2048]{0,1:T(8,128)(2,1)S(1)} %collective-permute-done.6), channel_id=1, source_target_pairs={{0,2},{2,4},{4,6},{6,8},{8,10},{10,12},{12,14},{14,16},{16,18},{18... | collective-permute-start | bytes 589832 | tf_op jit(solution)/shard_map/ppermute | solution.py:31
  131.2 14.2 %collective-permute-start.9 = (bf16[48,2048]{0,1:T(8,128)(2,1)S(1)}, bf16[48,2048]{0,1:T(8,128)(2,1)S(1)}, u32[]{:S(2)}, u32[]{:S(2)}) collective-permute-start(bf16[48,2048]{0,1:T(8,128)(2,1)S(1)} %collective-permute-done.7), channel_id=1, source_target_pairs={{0,30},{2,0},{4,2},{6,4},{8,6},{10,8},{12,10},{14,12},{16,14},{18,... | collective-permute-start | bytes 589832 | tf_op jit(solution)/shard_map/ppermute | solution.py:38
  138.4 11.4 %collective-permute-start.10 = (bf16[48,2048]{0,1:T(8,128)(2,1)S(1)}, bf16[48,2048]{0,1:T(8,128)(2,1)S(1)}, u32[]{:S(2)}, u32[]{:S(2)}) collective-permute-start(bf16[48,2048]{0,1:T(8,128)(2,1)S(1)} %collective-permute-done.8), channel_id=1, source_target_pairs={{0,2},{2,4},{4,6},{6,8},{8,10},{10,12},{12,14},{14,16},{16,18},{18... | collective-permute-start | bytes 589832 | tf_op jit(solution)/shard_map/ppermute | solution.py:31
  145.5 14.2 %collective-permute-start.11 = (bf16[48,2048]{0,1:T(8,128)(2,1)S(1)}, bf16[48,2048]{0,1:T(8,128)(2,1)S(1)}, u32[]{:S(2)}, u32[]{:S(2)}) collective-permute-start(bf16[48,2048]{0,1:T(8,128)(2,1)S(1)} %collective-permute-done.9), channel_id=1, source_target_pairs={{0,30},{2,0},{4,2},{6,4},{8,6},{10,8},{12,10},{14,12},{16,14},{18,... | collective-permute-start | bytes 589832 | tf_op jit(solution)/shard_map/ppermute | solution.py:38
  149.8 12.7 %collective-permute-start.12 = (bf16[48,2048]{0,1:T(8,128)(2,1)S(1)}, bf16[48,2048]{0,1:T(8,128)(2,1)S(1)}, u32[]{:S(2)}, u32[]{:S(2)}) collective-permute-start(bf16[48,2048]{0,1:T(8,128)(2,1)S(1)} %collective-permute-done.10), channel_id=1, source_target_pairs={{0,2},{2,4},{4,6},{6,8},{8,10},{10,12},{12,14},{14,16},{16,18},{18... | collective-permute-start | bytes 589832 | tf_op jit(solution)/shard_map/ppermute | solution.py:31
  159.7 14.2 %collective-permute-start.13 = (bf16[48,2048]{0,1:T(8,128)(2,1)S(1)}, bf16[48,2048]{0,1:T(8,128)(2,1)}, u32[]{:S(2)}, u32[]{:S(2)}) collective-permute-start(bf16[48,2048]{0,1:T(8,128)(2,1)S(1)} %collective-permute-done.11), channel_id=1, source_target_pairs={{0,30},{2,0},{4,2},{6,4},{8,6},{10,8},{12,10},{14,12},{16,14},{18,... | collective-permute-start | bytes 589832 | tf_op jit(solution)/shard_map/ppermute | solution.py:38
  162.5 14.3 %collective-permute-start.14 = (bf16[48,2048]{0,1:T(8,128)(2,1)S(1)}, bf16[48,2048]{0,1:T(8,128)(2,1)}, u32[]{:S(2)}, u32[]{:S(2)}) collective-permute-start(bf16[48,2048]{0,1:T(8,128)(2,1)S(1)} %collective-permute-done.12), channel_id=1, source_target_pairs={{0,2},{2,4},{4,6},{6,8},{8,10},{10,12},{12,14},{14,16},{16,18},{18... | collective-permute-start | bytes 589832 | tf_op jit(solution)/shard_map/ppermute | solution.py:31
  173.9 104.0 %collective-permute-start.15 = (bf16[48,2048]{0,1:T(8,128)(2,1)}, bf16[48,2048]{0,1:T(8,128)(2,1)}, u32[]{:S(2)}, u32[]{:S(2)}) collective-permute-start(bf16[48,2048]{0,1:T(8,128)(2,1)} %collective-permute-done.13), channel_id=1, source_target_pairs={{0,30},{2,0},{4,2},{6,4},{8,6},{10,8},{12,10},{14,12},{16,14},{18,... | collective-permute-start | bytes 589832 | tf_op jit(solution)/shard_map/ppermute | solution.py:38
  176.8 108.0 %collective-permute-start.16 = (bf16[48,2048]{0,1:T(8,128)(2,1)}, bf16[48,2048]{0,1:T(8,128)(2,1)}, u32[]{:S(2)}, u32[]{:S(2)}) collective-permute-start(bf16[48,2048]{0,1:T(8,128)(2,1)} %collective-permute-done.14), channel_id=1, source_target_pairs={{0,2},{2,4},{4,6},{6,8},{8,10},{10,12},{12,14},{14,16},{16,18},{18... | collective-permute-start | bytes 589832 | tf_op jit(solution)/shard_map/ppermute | solution.py:31
  305.5 117.8 %all-gather.3.cloned.1.call-start = ((), (), s32[]{:S(2)}) async-start(), calls=%async_computation.2 | async-start | bytes 3342336 | tf_op jit(solution)/shard_map/all_gather | solution.py:137
  379.1 91.4 %all-gather.5.cloned.1.call-start = ((), (), s32[]{:S(2)}) async-start(), calls=%async_computation.3 | async-start | bytes 3342336 | tf_op jit(solution)/shard_map/all_gather | solution.py:147
  380.0 123.4 %all-reduce.7.cloned.1.call-start = ((), (), s32[]{:S(2)}) async-start(), calls=%async_computation.6 | async-start | bytes 1179648 | tf_op jit(solution)/shard_map/psum | solution.py:174
  474.3 99.6 %reduce-scatter.9.cloned.1.call-start = ((), (), s32[]{:S(2)}) async-start(), calls=%async_computation.5 | async-start | bytes 3342336
  647.4 15.8 %collective-permute-start.17 = (bf16[48,1,3,128]{3,2,1,0:T(4,128)(2,1)S(1)}, bf16[48,1,3,128]{3,2,1,0:T(4,128)(2,1)S(1)}, u32[]{:S(2)}, u32[]{:S(2)}) collective-permute-start(bf16[48,1,3,128]{3,2,1,0:T(4,128)(2,1)S(1)} %get-tuple-element.85), channel_id=1, source_target_pairs={{0,1},{2,3},{4,5},{6,7},{8,9},{10,11},{12,13},{14,15},{16,17},{18,... | collective-permute-start | bytes 110600 | tf_op jit(solution)/shard_map/ppermute | solution.py:52
  650.8 12.4 %collective-permute-start.18 = (bf16[48,1,3,128]{3,2,1,0:T(4,128)(2,1)S(1)}, bf16[48,1,3,128]{3,2,1,0:T(4,128)(2,1)S(1)}, u32[]{:S(2)}, u32[]{:S(2)}) collective-permute-start(bf16[48,1,3,128]{3,2,1,0:T(4,128)(2,1)S(1)} %get-tuple-element.86), channel_id=1, source_target_pairs={{1,0},{3,2},{5,4},{7,6},{9,8},{11,10},{13,12},{15,14},{17,16},{19,... | collective-permute-start | bytes 110600 | tf_op jit(solution)/shard_map/ppermute | solution.py:55
  (102 other events, 1861.8 us)
Sparse Core Ops, SparseCore 0:
  305.6 66.5 reduce-scatter.6
  379.2 44.0 all-gather.2
  426.2 44.2 all-gather.4
  474.4 29.0 all-reduce.6
  507.6 66.2 reduce-scatter.8
